TPU v7x, 32 devices: a whole 2x2x4 slice. The times are simulated.
32 devices in a mesh: dp: 2 (over core), ctx: 4 (over y, x), hd: 4 (over z).
Axes of the slice: x: 2, y: 2, z: 4, core: 2. Of those that a mesh axis runs over, the one named last changes fastest.
Arguments:
- tokens_in: bfloat16 [4, 2048, 1536], P('dp', ('ctx', 'hd')), may hold values from -6 to 6
- seg_ids: int32 [4, 2048], P('dp'), may hold values from 0 to 7, never falling along the last dimension, each value on 1 to 512 neighbouring positions
- in_norm: float32 [1536], replicated, may hold values from 0.5 to 1.5
- z_proj: bfloat16 [1536, 3072], P(('dp', 'ctx', 'hd')), may hold values from -0.15625 to 0.15625
- xbc_proj: bfloat16 [1536, 3328], P(('dp', 'ctx', 'hd')), may hold values from -0.15625 to 0.15625
- dt_proj: bfloat16 [1536, 48], P(('dp', 'ctx', 'hd')), may hold values from -0.0390625 to 0.0390625
- conv_taps: float32 [4, 3328], replicated, may hold values from -3 to 3
- conv_bias: float32 [3328], replicated, may hold values from -2 to 2
- dt_bias: float32 [48], replicated, may hold values from -9 to -2
- a_log: float32 [48], replicated, may hold values from 0 to 2.77
- d_skip: float32 [48], replicated, may hold values from 0.5 to 2
- gate_norm: float32 [3072], replicated, may hold values from 0.5 to 1.5
- out_proj: bfloat16 [3072, 1536], P(('dp', 'ctx', 'hd')), may hold values from -0.109375 to 0.109375
- out_cotangent: bfloat16 [4, 2048, 1536], P('dp', ('ctx', 'hd')), may hold values from -6 to 6
Outputs:
- layer_out: bfloat16 [4, 2048, 1536], P('dp', ('ctx', 'hd'))
- tokens_grad: float32 [4, 2048, 1536], P('dp', ('ctx', 'hd'))
- in_norm_grad: float32 [1536], replicated
- z_proj_grad: float32 [1536, 3072], P(('dp', 'ctx', 'hd'))
- xbc_proj_grad: float32 [1536, 3328], P(('dp', 'ctx', 'hd'))
- dt_proj_grad: float32 [1536, 48], P(('dp', 'ctx', 'hd'))
- conv_taps_grad: float32 [4, 3328], replicated
- conv_bias_grad: float32 [3328], replicated
- dt_bias_grad: float32 [48], replicated
- a_log_grad: float32 [48], replicated
- d_skip_grad: float32 [48], replicated
- gate_norm_grad: float32 [3072], replicated
- out_proj_grad: float32 [3072, 1536], P(('dp', 'ctx', 'hd'))
Inputs may be any that keep to these rules, and one draw needn't show every extreme that they name: `seg_ids`: along each sequence the document numbers never fall; each document has 1 to 512 tokens and one has exactly that many.
All inputs are finite; a program needn't handle non-finite values.
Results may differ from a plain program's by a relative error of at most 0.0097.
Values may be sent and summed in bfloat16 or wider, within the bound.
No kernel may reach another device: no remote copies, remote signals or barrier semaphores. Data moves between devices by JAX's collectives and lax.ppermute only.
A program may use at most 320 MiB of HBM per device.

v0:
```python
import jax
import jax.numpy as jnp
from jax import lax
from jax.sharding import PartitionSpec as P

H = 48
P_SIZE = 64
N = 128
KW = 4
Q = 256
DI = 3072
HIGH = lax.Precision.HIGHEST
EPS = 1e-05


def from_behind(shard, axis, by):
    count = lax.axis_size(axis)
    pairs = [(i, i + by) for i in range(count) if 0 <= i + by < count]
    return lax.ppermute(shard, axis, pairs)


def carried_in(shard, axis, combine, identity, reverse):
    count, place = (lax.axis_size(axis), lax.axis_index(axis))
    everything = jax.tree.map(
        lambda part, kind: lax.all_gather(part.astype(kind), axis),
        shard,
        (jnp.bfloat16, jnp.bfloat16),
    )
    start = jax.tree.map(
        lambda part, zero: jnp.broadcast_to(jnp.asarray(zero, part.dtype), part.shape),
        shard,
        identity,
    )

    def turn(k, before):
        at = count - 1 - k if reverse else k
        reached = at > place if reverse else at < place
        new = combine(
            before, jax.tree.map(lambda part, own: part[at].astype(own.dtype), everything, shard)
        )
        return jax.tree.map(lambda a, b: jnp.where(reached, a, b), new, before)

    return lax.fori_loop(0, count, turn, start)


def norm_rows(values, gain):
    return values * lax.rsqrt(jnp.mean(values * values, axis=-1, keepdims=True) + EPS) * gain


def gate_tail(mixer_val, gate_val, gain):
    return norm_rows(mixer_val * jax.nn.silu(gate_val), gain)


def conv_act(padded, taps, bias, masks):
    length = masks.shape[1]
    mixed = bias
    for tap in range(taps.shape[0]):
        mixed = mixed + taps[tap] * padded[tap : tap + length] * masks[tap][:, None]
    return jax.nn.silu(mixed)


def back_dot(grad_val, weight):
    return lax.dot_general(
        grad_val, weight, (((1,), (1,)), ((), ())), preferred_element_type=jnp.float32
    )


def compose(earlier, later):
    return (earlier[0] * later[0], later[0][:, None, None] * earlier[1] + later[1])


def block_decay(rate_val, bias_here, decay_log, seg_blk, seg_before):
    log_rate = jax.nn.softplus(rate_val + bias_here) * -jnp.exp(decay_log)
    cumul = jnp.cumsum(log_rate, axis=0)
    keep = (seg_blk == seg_before).astype(jnp.float32)
    lead = jnp.exp(cumul) * keep[:, None]
    return (lead[-1], lead)


def block_ssd(
    x_val,
    rate_val,
    bias_here,
    decay_log,
    skip_here,
    bc_val,
    state_in,
    seg_blk,
    seg_before,
    span_len,
):
    length, heads = rate_val.shape
    count = length // span_len
    width_n = bc_val.shape[1] // 2
    x_groups = x_val.reshape(count, span_len, heads, -1)
    dt_groups = jax.nn.softplus(rate_val + bias_here).reshape(count, span_len, heads)
    cumul = jnp.cumsum(dt_groups * -jnp.exp(decay_log), axis=1)
    b_groups = bc_val[:, :width_n].reshape(count, span_len, width_n)
    c_groups = bc_val[:, width_n:].reshape(count, span_len, width_n)
    seg_groups = seg_blk.reshape(count, span_len)
    before = jnp.concatenate([seg_before, seg_groups[:-1, -1]])
    order = jnp.arange(span_len)
    mask = (seg_groups[:, :, None] == seg_groups[:, None, :]) & (order[:, None] >= order[None, :])
    gaps = cumul[:, :, None, :] - cumul[:, None, :, :]
    decay = jnp.exp(jnp.where(mask[..., None], gaps, 0.0)) * mask[..., None].astype(jnp.float32)
    scores = jnp.einsum("ctn,csn->cts", c_groups, b_groups, precision=HIGH)
    mix_w = scores[..., None] * decay * dt_groups[:, None, :, :]
    y_part = jnp.einsum("ctsh,cshp->cthp", mix_w, x_groups, precision=HIGH)
    keep = (seg_groups == before[:, None]).astype(jnp.float32)
    lead = jnp.exp(cumul) * keep[..., None]
    tail = (
        jnp.exp(cumul[:, -1:, :] - cumul)
        * (seg_groups == seg_groups[:, -1:]).astype(jnp.float32)[..., None]
        * dt_groups
    )
    pieces = jnp.einsum("csh,cshp,csn->chpn", tail, x_groups, b_groups, precision=HIGH)

    def advance(state, item):
        piece, factor = item
        return (state * factor[:, None, None] + piece, state)

    state_end, entering = lax.scan(advance, state_in, (pieces, lead[:, -1, :]))
    y_part = y_part + lead[..., None] * jnp.einsum(
        "ctn,chpn->cthp", c_groups, entering, precision=HIGH
    )
    y_part = y_part + skip_here[:, None] * x_groups
    return (y_part.reshape(length, -1), state_end)


def shards(
    tokens_in,
    seg_ids,
    in_norm,
    z_proj,
    xbc_proj,
    dt_proj,
    conv_taps,
    conv_bias,
    dt_bias,
    a_log,
    d_skip,
    gate_norm,
    out_proj,
    out_cotangent,
):
    batches, rows, width = tokens_in.shape
    n_heads_axis = lax.axis_size("hd")
    heads_here = H // n_heads_axis
    block = rows * n_heads_axis
    channels = DI + 2 * N
    start_tok = lax.axis_index(("ctx", "hd")) * rows
    start_blk = lax.axis_index("ctx") * block
    head_low = lax.axis_index("hd") * heads_here
    bias_here = lax.dynamic_slice_in_dim(dt_bias, head_low, heads_here)
    decay_log = lax.dynamic_slice_in_dim(a_log, head_low, heads_here)
    skip_here = lax.dynamic_slice_in_dim(d_skip, head_low, heads_here)
    unit = (jnp.ones((heads_here,), jnp.float32), jnp.zeros((heads_here, P_SIZE, N), jnp.float32))

    def fetch():
        return (
            lax.all_gather(z_proj, ("dp", "ctx", "hd"), axis=0, tiled=True),
            lax.all_gather(xbc_proj, ("dp", "ctx", "hd"), axis=0, tiled=True),
            lax.all_gather(dt_proj, ("dp", "ctx", "hd"), axis=0, tiled=True),
            lax.all_gather(out_proj, ("dp", "ctx", "hd"), axis=0, tiled=True),
        )

    stored = []
    outputs = []
    for batch in range(batches):
        zed_weight, xbc_weight, rate_weight, out_weight = fetch()
        seg_row = seg_ids[batch]
        seg_pad = jnp.concatenate([jnp.full((KW - 1,), -1, jnp.int32), seg_row])
        seg_near = lax.dynamic_slice_in_dim(seg_pad, start_tok, rows + KW - 1)
        seg_own = seg_near[KW - 1 :]
        masks = jnp.stack([seg_near[tap : tap + rows] == seg_own for tap in range(KW)]).astype(
            jnp.float32
        )
        seg_blk = lax.dynamic_slice_in_dim(seg_row, start_blk, block)
        seg_before = lax.dynamic_slice_in_dim(seg_pad, start_blk + KW - 2, 1)
        source = tokens_in[batch].astype(jnp.float32)
        normed = norm_rows(source, in_norm).astype(jnp.bfloat16)
        gate_in = jnp.dot(normed, zed_weight, preferred_element_type=jnp.float32)
        raw_xbc = jnp.dot(normed, xbc_weight, preferred_element_type=jnp.float32).astype(
            jnp.bfloat16
        )
        rate_raw = jnp.dot(normed, rate_weight, preferred_element_type=jnp.float32).astype(
            jnp.bfloat16
        )
        rim_rows = from_behind(raw_xbc[rows - (KW - 1) :], ("ctx", "hd"), 1)
        padded = jnp.concatenate([rim_rows, raw_xbc], 0).astype(jnp.float32)
        active = conv_act(padded, conv_taps, conv_bias, masks)
        x_low = active[:, :DI].astype(jnp.bfloat16)
        bc_low = active[:, DI:].astype(jnp.bfloat16)
        x_heads, rate_heads = (
            lax.all_to_all(x_low, "hd", split_axis=1, concat_axis=0, tiled=True),
            lax.all_to_all(rate_raw, "hd", split_axis=1, concat_axis=0, tiled=True),
        )
        bc_all = lax.all_gather(bc_low, "hd", axis=0, tiled=True)
        x_float = x_heads.astype(jnp.float32)
        rate_float = rate_heads.astype(jnp.float32)
        bc_float = bc_all.astype(jnp.float32)
        zero_state = jnp.zeros((heads_here, P_SIZE, N), jnp.float32)
        y_zero, state_local = block_ssd(
            x_float,
            rate_float,
            bias_here,
            decay_log,
            skip_here,
            bc_float,
            zero_state,
            seg_blk,
            seg_before,
            Q,
        )
        total_decay, lead_blk = block_decay(rate_float, bias_here, decay_log, seg_blk, seg_before)
        unused, state_in = carried_in((total_decay, state_local), "ctx", compose, unit, False)
        carried = lead_blk[:, :, None] * jnp.einsum(
            "tn,hpn->thp", bc_float[:, N:], state_in, precision=HIGH
        )
        y_heads = y_zero + carried.reshape(block, -1)
        y_tokens = lax.all_to_all(
            y_heads.astype(jnp.bfloat16), "hd", split_axis=0, concat_axis=1, tiled=True
        )
        y_float = y_tokens.astype(jnp.float32)
        gated = gate_tail(y_float, gate_in, gate_norm).astype(jnp.bfloat16)
        result = source + jnp.dot(gated, out_weight, preferred_element_type=jnp.float32)
        outputs.append(result.astype(jnp.bfloat16))
        stored.append(
            (
                source,
                normed,
                gate_in,
                padded,
                masks,
                x_float,
                rate_float,
                bc_float,
                seg_blk,
                seg_before,
                lead_blk,
                total_decay,
                state_in,
                y_float,
                gated,
            )
        )
    grads_tok = []
    normed_rows = []
    proj_grads = []
    gated_rows = []
    cot_rows = []
    norm_total = jnp.zeros((width,), jnp.float32)
    taps_total = jnp.zeros(conv_taps.shape, jnp.float32)
    cbias_total = jnp.zeros((channels,), jnp.float32)
    dtb_total = jnp.zeros((H,), jnp.float32)
    alog_total = jnp.zeros((H,), jnp.float32)
    skip_total = jnp.zeros((H,), jnp.float32)
    gate_total = jnp.zeros((DI,), jnp.float32)
    for batch in range(batches):
        zed_weight, xbc_weight, rate_weight, out_weight = fetch()
        (
            source,
            normed,
            gate_in,
            padded,
            masks,
            x_float,
            rate_float,
            bc_float,
            seg_blk,
            seg_before,
            lead_blk,
            total_decay,
            state_in,
            y_float,
            gated,
        ) = stored[batch]
        cot_low = out_cotangent[batch]
        d_gated = back_dot(cot_low, out_weight)
        unused, tail_pull = jax.vjp(gate_tail, y_float, gate_in, gate_norm)
        d_mixer, d_gate_in, d_gain = tail_pull(d_gated)
        d_mixer_heads = lax.all_to_all(
            d_mixer.astype(jnp.bfloat16), "hd", split_axis=1, concat_axis=0, tiled=True
        )
        d_y_float = d_mixer_heads.astype(jnp.float32)
        d_local = jnp.einsum(
            "th,thp,tn->hpn",
            lead_blk,
            d_y_float.reshape(block, heads_here, P_SIZE),
            bc_float[:, N:],
            precision=HIGH,
        )
        unused, d_end = carried_in((total_decay, d_local), "ctx", compose, unit, True)

        def with_state(x_value, rate_value, bias_value, decay_value, skip_value, bc_value):
            return block_ssd(
                x_value,
                rate_value,
                bias_value,
                decay_value,
                skip_value,
                bc_value,
                state_in,
                seg_blk,
                seg_before,
                Q,
            )

        unused, ssd_pull = jax.vjp(
            with_state, x_float, rate_float, bias_here, decay_log, skip_here, bc_float
        )
        d_x_heads, d_rate_heads, d_bias_h, d_decay_h, d_skip_h, d_bc_heads = ssd_pull(
            (d_y_float, d_end)
        )
        d_x_tok, d_rate_tok = (
            lax.all_to_all(
                d_x_heads.astype(jnp.bfloat16), "hd", split_axis=0, concat_axis=1, tiled=True
            ),
            lax.all_to_all(
                d_rate_heads.astype(jnp.bfloat16), "hd", split_axis=0, concat_axis=1, tiled=True
            ),
        )
        d_bc_tok = lax.psum_scatter(
            d_bc_heads.astype(jnp.bfloat16), "hd", scatter_dimension=0, tiled=True
        ).astype(jnp.float32)
        d_active = jnp.concatenate([d_x_tok.astype(jnp.float32), d_bc_tok], axis=1)

        def conv_here(pad_value, taps_value, bias_value):
            return conv_act(pad_value, taps_value, bias_value, masks)

        unused, conv_pull = jax.vjp(conv_here, padded, conv_taps, conv_bias)
        d_padded, d_taps, d_cbias = conv_pull(d_active)
        back_rim = from_behind(d_padded[: KW - 1].astype(jnp.bfloat16), ("ctx", "hd"), -1).astype(
            jnp.float32
        )
        d_raw = d_padded[KW - 1 :] + jnp.concatenate(
            [jnp.zeros((rows - (KW - 1), channels), jnp.float32), back_rim], 0
        )
        d_raw_low = d_raw.astype(jnp.bfloat16)
        d_gate_low = d_gate_in.astype(jnp.bfloat16)
        d_normed = (
            back_dot(d_gate_low, zed_weight)
            + back_dot(d_raw_low, xbc_weight)
            + back_dot(d_rate_tok, rate_weight)
        )
        unused, norm_pull = jax.vjp(norm_rows, source, in_norm)
        d_source, d_norm_gain = norm_pull(d_normed)
        grads_tok.append(d_source + cot_low.astype(jnp.float32))
        normed_rows.append(normed)
        proj_grads.append(jnp.concatenate([d_gate_low, d_raw_low, d_rate_tok], axis=1))
        gated_rows.append(gated)
        cot_rows.append(cot_low)
        norm_total = norm_total + d_norm_gain
        taps_total = taps_total + d_taps
        cbias_total = cbias_total + d_cbias
        dtb_total = dtb_total + lax.dynamic_update_slice_in_dim(
            jnp.zeros((H,), jnp.float32), d_bias_h, head_low, 0
        )
        alog_total = alog_total + lax.dynamic_update_slice_in_dim(
            jnp.zeros((H,), jnp.float32), d_decay_h, head_low, 0
        )
        skip_total = skip_total + lax.dynamic_update_slice_in_dim(
            jnp.zeros((H,), jnp.float32), d_skip_h, head_low, 0
        )
        gate_total = gate_total + d_gain
    normed_all = jnp.concatenate(normed_rows, 0)
    proj_all = jnp.concatenate(proj_grads, 0)
    gated_all = jnp.concatenate(gated_rows, 0)
    cot_all = jnp.concatenate(cot_rows, 0)
    part = normed_all
    in_grad = lax.psum_scatter(
        lax.dot_general(
            part, proj_all, (((0,), (0,)), ((), ())), preferred_element_type=jnp.float32
        ),
        ("dp", "ctx", "hd"),
        scatter_dimension=0,
        tiled=True,
    )
    part = gated_all
    out_grad = lax.psum_scatter(
        lax.dot_general(
            part, cot_all, (((0,), (0,)), ((), ())), preferred_element_type=jnp.float32
        ),
        ("dp", "ctx", "hd"),
        scatter_dimension=0,
        tiled=True,
    )
    norm_sum, taps_sum, cbias_sum, dtb_sum, alog_sum, skip_sum, gate_sum = lax.psum(
        (norm_total, taps_total, cbias_total, dtb_total, alog_total, skip_total, gate_total),
        ("dp", "ctx", "hd"),
    )
    return (
        jnp.stack(outputs),
        jnp.stack(grads_tok),
        norm_sum,
        in_grad[:, :DI],
        in_grad[:, DI : DI + channels],
        in_grad[:, DI + channels :],
        taps_sum,
        cbias_sum,
        dtb_sum,
        alog_sum,
        skip_sum,
        gate_sum,
        out_grad,
    )


def solution(mesh):
    in_specs = (
        P("dp", ("ctx", "hd"), None),
        P("dp", None),
        P(),
        P(("dp", "ctx", "hd"), None),
        P(("dp", "ctx", "hd"), None),
        P(("dp", "ctx", "hd"), None),
        P(),
        P(),
        P(),
        P(),
        P(),
        P(),
        P(("dp", "ctx", "hd"), None),
        P("dp", ("ctx", "hd"), None),
    )
    out_specs = (
        P("dp", ("ctx", "hd"), None),
        P("dp", ("ctx", "hd"), None),
        P(),
        P(("dp", "ctx", "hd"), None),
        P(("dp", "ctx", "hd"), None),
        P(("dp", "ctx", "hd"), None),
        P(),
        P(),
        P(),
        P(),
        P(),
        P(),
        P(("dp", "ctx", "hd"), None),
    )
    return jax.shard_map(shards, mesh=mesh, in_specs=in_specs, out_specs=out_specs, check_vma=False)
```

profile of v0, /device:TPU:0, one launch (start us, length us, event | category | flops | bytes accessed | tf_op | source)
XLA Modules:
  0.0 1491.1 jit_solution(12795185626710274791)
XLA Ops:
  8.7 76.8 %all_gather.68 = bf16[1536,48]{1,0:T(8,128)(2,1)S(1)} all-gather(bf16[48,48]{1,0:T(8,128)(2,1)} %param.40), channel_id=1, replica_groups=mesh['dp'=2,'ctx'=4,'hd'=4] {'dp','ctx','hd'}, dimensions={0}, use_global_device_ids=true | all-gather | bytes 152064 | tf_op jit(solution)/shard_map/all_gather | solution.py:163
  125.4 14.0 all-gather.5
  188.7 17.7 %all_gather.74 = bf16[512,256]{1,0:T(8,128)(2,1)S(1)} all-gather(bf16[128,256]{1,0:T(8,128)(2,1)S(1)} %slice.403), channel_id=1, replica_groups=mesh['dp'=2,'ctx'=4,'hd'=4] {'hd'}, dimensions={0}, use_global_device_ids=true | all-gather | bytes 327680 | tf_op jit(solution)/shard_map/all_gather | solution.py:198
  206.4 15.0 %all_gather.33 = bf16[512,256]{1,0:T(8,128)(2,1)S(1)} all-gather(bf16[128,256]{1,0:T(8,128)(2,1)S(1)} %slice.386), channel_id=1, replica_groups=mesh['dp'=2,'ctx'=4,'hd'=4] {'hd'}, dimensions={0}, use_global_device_ids=true | all-gather | bytes 327680 | tf_op jit(solution)/shard_map/all_gather | solution.py:198
  238.3 7.7 while.156
  247.1 12.9 all-gather.1
  289.1 14.6 all-to-all-start.5
  313.3 7.6 while.154
  321.9 11.6 all-gather
  401.5 9.2 multiply_reduce_fusion.13
  418.0 9.1 multiply_convert_fusion.3
  446.5 13.0 all-to-all-done.9
  472.3 10.0 all-gather.3
  495.6 7.8 while.153
  524.5 12.2 all-gather.2
  708.2 16.6 %reduce-scatter.5.cloned.1.call-done = bf16[128,256]{1,0:T(8,128)(2,1)} async-done(((bf16[512,256]{1,0:T(8,128)(2,1)}), bf16[128,256]{1,0:T(8,128)(2,1)}) %reduce-scatter.5.cloned.1.call-update) | async-done | bytes 65552 | tf_op jit(solution)/shard_map/reduce_scatter | solution.py:323
  741.9 19.9 %fusion.38 = f32[1536,6448]{1,0:T(8,128)} fusion(bf16[128,48]{1,0:T(8,128)(2,1)S(1)} %copy.500, bf16[128,3328]{1,0:T(8,128)(2,1)S(1)} %fusion.98, bf16[128,3072]{1,0:T(8,128)(2,1)S(1)} %copy-done.28, bf16[128,48]{1,0:T(8,128)(2,1)S(1)} %copy-done.103, bf16[128,3328]{1,0:T(8,128)(2,1)S(1)} %fusion.99, bf16[128,3072]{1,0:T(8,128)(2,1)} %get-tuple-element.1175, ...), kind=kOutput, calls=%fused_computation.78 | convolution fusion | flops 5092294656 | bytes 43704320 | tf_op jit(solution)/shard_map/dot_general | solution.py:372
  771.4 9.5 fusion.276
  788.5 8.9 convolution_add_fusion.2
  798.7 9.0 convolution_add_fusion.3
  809.9 11.9 fusion.118
  836.5 293.6 %reduce-scatter.9.cloned.1.call-done = f32[48,6448]{1,0:T(8,128)} async-done(((f32[1536,6448]{1,0:T(8,128)}), f32[48,6448]{1,0:T(8,128)}) %reduce-scatter.9.cloned.1.call-update) | async-done | bytes 1238032 | tf_op jit(solution)/shard_map/reduce_scatter | solution.py:371
  1135.3 125.0 %all-reduce.31.cloned.1.call-done = (f32[1536]{0:T(1024)}, f32[4,3328]{1,0:T(4,128)}, f32[3328]{0:T(1024)}, f32[48]{0:T(128)}, f32[48]{0:T(128)}, /*index=5*/f32[48]{0:T(128)}, f32[3072]{0:T(1024)}) async-done(((f32[1536]{0:T(1024)}, f32[4,3328]{1,0:T(4,128)}, f32[3328]{0:T(1024)}, f32[48]{0:T(128)}, f32[48]{0:T(128)}, /*index=5*/f32[48]{0:T(128)}, f32[3072]{0:T(1024)}), (f32[1536]{0:T(1024)}, ...) | async-done | bytes 85584 | tf_op jit(solution)/shard_map/psum | solution.py:388
  1260.2 214.8 %reduce-scatter.11.cloned.1.call-done = f32[96,1536]{1,0:T(8,128)} async-done(((f32[3072,1536]{1,0:T(8,128)}), f32[96,1536]{1,0:T(8,128)}) %reduce-scatter.11.cloned.1.call-update) | async-done | bytes 589840 | tf_op jit(solution)/shard_map/reduce_scatter | solution.py:380
  (854 shorter events, 586.1 us)
Async XLA Ops:
  7.2 145.4 %all-gather.10.cloned.1.call-start = ((), (), s32[]{:S(2)}) async-start(), calls=%async_computation.16 | async-start | bytes 10543104 | tf_op jit(solution)/shard_map/all_gather | solution.py:162
  7.9 385.7 %all-gather.12.cloned.1.call-start = ((), (), s32[]{:S(2)}) async-start(), calls=%async_computation.17 | async-start | bytes 9732096 | tf_op jit(solution)/shard_map/all_gather | solution.py:161
  88.8 16.4 %all-to-all-start.4 = ((bf16[128,4,12]{0,2,1:T(8,128)(2,1)}), bf16[128,4,12]{0,2,1:T(8,128)(2,1)S(1)}, u32[]{:S(2)}, u32[]{:S(2)}) async-start(bf16[128,4,12]{0,2,1:T(8,128)(2,1)} %all_to_all.141), calls=%async_computation.4 | async-start | bytes 32768 | tf_op jit(solution)/shard_map/all_to_all | solution.py:196
  92.1 309.4 %all-gather.14.cloned.1.call-start = ((), (), s32[]{:S(2)}) async-start(), calls=%async_computation.18 | async-start | bytes 9732096 | tf_op jit(solution)/shard_map/all_gather | solution.py:164
  105.2 10.8 all-to-all-start.1
  159.3 7.4 collective-permute-start.1
  164.6 15.9 %collective-permute-start = (bf16[3,3328]{1,0:T(4,128)(2,1)}, bf16[3,3328]{1,0:T(4,128)(2,1)S(1)}, u32[]{:S(2)}, u32[]{:S(2)}) collective-permute-start(bf16[3,3328]{1,0:T(4,128)(2,1)} %slice.380), channel_id=1, source_target_pairs={{0,1},{1,2},{2,3},{3,4},{4,5},{5,6},{6,7},{7,8},{8,9},{9,10},{10,1... | collective-permute-start | bytes 59912 | tf_op jit(solution)/shard_map/ppermute | solution.py:19
  173.7 50.4 %all-to-all-start.3 = ((bf16[128,4,768]{0,2,1:T(8,128)(2,1)}), bf16[128,4,768]{0,2,1:T(8,128)(2,1)}, u32[]{:S(2)}, u32[]{:S(2)}) async-start(bf16[128,4,768]{0,2,1:T(8,128)(2,1)} %bitcast.581), calls=%async_computation.3 | async-start | bytes 1572864 | tf_op jit(solution)/shard_map/all_to_all | solution.py:195
  224.1 64.9 %all-to-all-start = ((bf16[128,4,768]{0,2,1:T(8,128)(2,1)}), bf16[128,4,768]{0,2,1:T(8,128)(2,1)}, u32[]{:S(2)}, u32[]{:S(2)}) async-start(bf16[128,4,768]{0,2,1:T(8,128)(2,1)} %bitcast.579), calls=%async_computation | async-start | bytes 1572864 | tf_op jit(solution)/shard_map/all_to_all | solution.py:195
  289.1 80.1 %all-to-all-start.5 = ((bf16[4,128,768]{1,2,0:T(8,128)(2,1)}), bf16[4,128,768]{1,2,0:T(8,128)(2,1)}, u32[]{:S(2)}, u32[]{:S(2)}) async-start(bf16[4,128,768]{1,2,0:T(8,128)(2,1)} %copy.441), calls=%async_computation.5 | async-start | bytes 1572864 | tf_op jit(solution)/shard_map/all_to_all | solution.py:221
  369.2 18.9 %all-to-all-start.2 = ((bf16[4,128,768]{1,2,0:T(8,128)(2,1)}), bf16[4,128,768]{1,2,0:T(8,128)(2,1)}, u32[]{:S(2)}, u32[]{:S(2)}) async-start(bf16[4,128,768]{1,2,0:T(8,128)(2,1)} %copy.425), calls=%async_computation.2 | async-start | bytes 1572864 | tf_op jit(solution)/shard_map/all_to_all | solution.py:221
  434.2 25.3 %all-to-all-start.9 = ((bf16[128,4,768]{0,2,1:T(8,128)(2,1)}), bf16[128,4,768]{0,2,1:T(8,128)(2,1)}, u32[]{:S(2)}, u32[]{:S(2)}) async-start(bf16[128,4,768]{0,2,1:T(8,128)(2,1)} %bitcast.580), calls=%async_computation.10 | async-start | bytes 1572864 | tf_op jit(solution)/shard_map/all_to_all | solution.py:282
  459.5 56.3 %all-to-all-start.6 = ((bf16[128,4,768]{0,2,1:T(8,128)(2,1)}), bf16[128,4,768]{0,2,1:T(8,128)(2,1)}, u32[]{:S(2)}, u32[]{:S(2)}) async-start(bf16[128,4,768]{0,2,1:T(8,128)(2,1)} %bitcast.84), calls=%async_computation.6 | async-start | bytes 1572864 | tf_op jit(solution)/shard_map/all_to_all | solution.py:282
  620.8 12.0 all-to-all-start.11
  632.9 15.1 %all-to-all-start.8 = ((bf16[4,128,12]{1,2,0:T(8,128)(2,1)}), bf16[4,128,12]{1,2,0:T(8,128)(2,1)}, u32[]{:S(2)}, u32[]{:S(2)}) async-start(bf16[4,128,12]{1,2,0:T(8,128)(2,1)} %copy.470), calls=%async_computation.9 | async-start | bytes 32768 | tf_op jit(solution)/shard_map/all_to_all | solution.py:319
  648.0 27.4 %all-to-all-start.10 = ((bf16[4,128,768]{1,2,0:T(8,128)(2,1)}), bf16[4,128,768]{1,2,0:T(8,128)(2,1)}, u32[]{:S(2)}, u32[]{:S(2)}) async-start(bf16[4,128,768]{1,2,0:T(8,128)(2,1)} %copy.484), calls=%async_computation.11 | async-start | bytes 1572864 | tf_op jit(solution)/shard_map/all_to_all | solution.py:316
  675.4 21.7 %all-to-all-start.7 = ((bf16[4,128,768]{1,2,0:T(8,128)(2,1)}), bf16[4,128,768]{1,2,0:T(8,128)(2,1)}, u32[]{:S(2)}, u32[]{:S(2)}) async-start(bf16[4,128,768]{1,2,0:T(8,128)(2,1)} %copy.456), calls=%async_computation.7 | async-start | bytes 1572864 | tf_op jit(solution)/shard_map/all_to_all | solution.py:316
  680.6 23.5 %reduce-scatter.7.cloned.1.call-start = ((), (), s32[]{:S(2)}) async-start(), calls=%async_computation.20 | async-start | bytes 327680 | tf_op jit(solution)/shard_map/reduce_scatter | solution.py:323
  683.6 41.1 %reduce-scatter.5.cloned.1.call-start = ((), (), s32[]{:S(2)}) async-start(), calls=%async_computation.19 | async-start | bytes 327680 | tf_op jit(solution)/shard_map/reduce_scatter | solution.py:323
  692.4 437.6 %reduce-scatter.9.cloned.1.call-start = ((), (), s32[]{:S(2)}) async-start(), calls=%async_computation.21 | async-start | bytes 41361408 | tf_op jit(solution)/shard_map/reduce_scatter | solution.py:371
  733.4 5.8 collective-permute-start.3
  735.3 6.4 collective-permute-start.2
  761.8 498.5 %all-reduce.31.cloned.1.call-start = ((), (), s32[]{:S(2)}) async-start(), calls=%async_computation.23 | async-start | bytes 183296 | tf_op jit(solution)/shard_map/psum | solution.py:388
  809.9 665.2 %reduce-scatter.11.cloned.1.call-start = ((), (), s32[]{:S(2)}) async-start(), calls=%async_computation.22 | async-start | bytes 19464192 | tf_op jit(solution)/shard_map/reduce_scatter | solution.py:380
  (190 other events, 1944.6 us)
Sparse Core Ops, SparseCore 0:
  10.8 90.7 all-gather.9
  104.4 90.3 all-gather.11
  197.6 94.1 all-gather.13
  683.9 20.1 reduce-scatter.6
  706.8 17.8 reduce-scatter.4
  761.9 368.0 reduce-scatter.8
  1137.6 122.5 all-reduce.30
  1267.2 207.8 reduce-scatter.10
where the time goes:
time: 1500 us; the launch traced here: 1490 us
  waiting for transfers between devices  684 us (46%)
  matrix products  216 us (14%)
  local copies, waits for them, and re-layouts  179 us (12%)
  blocking collectives  177 us (12%)
  other arithmetic  140 us (9%)
  starting transfers between devices  77 us (5%)
  between operations  17.4 us (1%)
    reduce_scatter x1, waiting for transfers between devices, shards(): lax.psum_scatter(lax.dot_general(part, proj_all, (((0,), (0,)), ((), ()))...  294 us
    reduce_scatter x1, waiting for transfers between devices, shards(): lax.psum_scatter(lax.dot_general(part, cot_all, (((0,), (0,)), ((), ())),...  215 us
    psum x1, waiting for transfers between devices, shards(): lax.psum((norm_total, taps_total, cbias_total, dtb_total, alog_total, ski...  125 us
    all_gather x1, blocking collectives, fetch(): lax.all_gather(dt_proj, ('dp', 'ctx', 'hd'), axis=0, tiled=True)  76.8 us
    all_gather x6, blocking collectives, carried_in(): lax.all_gather(part.astype(kind), axis)  67.1 us
    dot_general x8, matrix products, back_dot(): lax.dot_general(grad_val, weight, (((1,), (1,)), ((), ())), preferred_ele...  54.5 us
    dot_general x6, matrix products, block_ssd(): y_part = jnp.einsum('ctsh,cshp->cthp', mix_w, x_groups, precision=HIGH)  37.6 us
    all_gather x2, blocking collectives, shards(): bc_all = lax.all_gather(bc_low, 'hd', axis=0, tiled=True)  32.6 us
  transfers between devices with their start and end apart: 24, of which 10 were waited for; matrix products, arithmetic and copies ran while one was open for 24% of the time, Pallas kernels for 0%

commit v1 on v0

--- a/solution.py
+++ b/solution.py
@@ -279,9 +279,21 @@
         d_gated = back_dot(cot_low, out_weight)
         unused, tail_pull = jax.vjp(gate_tail, y_float, gate_in, gate_norm)
         d_mixer, d_gate_in, d_gain = tail_pull(d_gated)
-        d_mixer_heads = lax.all_to_all(
-            d_mixer.astype(jnp.bfloat16), "hd", split_axis=1, concat_axis=0, tiled=True
-        )
+        array = d_mixer.astype(jnp.bfloat16)
+        ways, here = (lax.axis_size("hd"), lax.axis_index("hd"))
+        width_2 = array.shape[1] // ways
+        dims = list(array.shape)
+        dims[1] = width_2
+        height = dims[0]
+        dims[0] = height * ways
+        d_mixer_heads = jnp.zeros(dims, array.dtype)
+        for mask_2 in range(ways):
+            part_2 = lax.dynamic_slice_in_dim(array, (here ^ mask_2) * width_2, width_2, axis=1)
+            if mask_2:
+                part_2 = lax.ppermute(part_2, "hd", [(d, d ^ mask_2) for d in range(ways)])
+            d_mixer_heads = lax.dynamic_update_slice_in_dim(
+                d_mixer_heads, part_2, (here ^ mask_2) * height, axis=0
+            )
         d_y_float = d_mixer_heads.astype(jnp.float32)
         d_local = jnp.einsum(
             "th,thp,tn->hpn",

time: 1500 us -> 1460 us (0.973)
  local copies, waits for them, and re-layouts: 179 us -> 150 us
    all_to_all x6 -> x0, local copies, waits for them, and re-layouts: 15.9 us -> none  [shards(): lax.all_to_all(d_mixer.astype(jnp.bfloat16), 'hd', split_axis=1, concat_a...]
  transfers between devices with their start and end apart: 24 -> 28, of which waited for: 10 -> 10; matrix products, arithmetic and copies ran while one was open for 24% -> 22% of each run, Pallas kernels for 0% -> 0%
where the time goes in v1:
time: 1460 us; the launch traced here: 1450 us
  waiting for transfers between devices  683 us (47%)
  matrix products  213 us (15%)
  blocking collectives  180 us (12%)
  local copies, waits for them, and re-layouts  150 us (10%)
  other arithmetic  128 us (9%)
  starting transfers between devices  76.1 us (5%)
  between operations  17.6 us (1%)
    reduce_scatter x1, waiting for transfers between devices, shards(): lax.psum_scatter(lax.dot_general(part, proj_all, (((0,), (0,)), ((), ()))...  293 us
    reduce_scatter x1, waiting for transfers between devices, shards(): lax.psum_scatter(lax.dot_general(part, cot_all, (((0,), (0,)), ((), ())),...  215 us
    psum x1, waiting for transfers between devices, shards(): lax.psum((norm_total, taps_total, cbias_total, dtb_total, alog_total, ski...  125 us
    all_gather x1, blocking collectives, fetch(): lax.all_gather(dt_proj, ('dp', 'ctx', 'hd'), axis=0, tiled=True)  76.8 us
    all_gather x6, blocking collectives, carried_in(): lax.all_gather(part.astype(kind), axis)  65.9 us
    dot_general x8, matrix products, back_dot(): lax.dot_general(grad_val, weight, (((1,), (1,)), ((), ())), preferred_ele...  55.4 us
    dot_general x6, matrix products, block_ssd(): y_part = jnp.einsum('ctsh,cshp->cthp', mix_w, x_groups, precision=HIGH)  40.1 us
    all_gather x2, blocking collectives, shards(): bc_all = lax.all_gather(bc_low, 'hd', axis=0, tiled=True)  36.9 us
  transfers between devices with their start and end apart: 28, of which 10 were waited for; matrix products, arithmetic and copies ran while one was open for 22% of the time, Pallas kernels for 0%

profile of v1, /device:TPU:0, one launch (start us, length us, event | category | flops | bytes accessed | tf_op | source)
XLA Modules:
  0.0 1447.9 jit_solution(12907728612788583242)
XLA Ops:
  8.7 76.8 %all_gather.68 = bf16[1536,48]{1,0:T(8,128)(2,1)S(1)} all-gather(bf16[48,48]{1,0:T(8,128)(2,1)} %param.40), channel_id=1, replica_groups=mesh['dp'=2,'ctx'=4,'hd'=4] {'dp','ctx','hd'}, dimensions={0}, use_global_device_ids=true | all-gather | bytes 152064 | tf_op jit(solution)/shard_map/all_gather | solution.py:163
  125.0 14.3 all-gather.5
  184.4 21.9 %all_gather.74 = bf16[512,256]{1,0:T(8,128)(2,1)S(1)} all-gather(bf16[128,256]{1,0:T(8,128)(2,1)S(1)} %slice.403), channel_id=1, replica_groups=mesh['dp'=2,'ctx'=4,'hd'=4] {'hd'}, dimensions={0}, use_global_device_ids=true | all-gather | bytes 327680 | tf_op jit(solution)/shard_map/all_gather | solution.py:198
  206.3 15.0 %all_gather.33 = bf16[512,256]{1,0:T(8,128)(2,1)S(1)} all-gather(bf16[128,256]{1,0:T(8,128)(2,1)S(1)} %slice.386), channel_id=1, replica_groups=mesh['dp'=2,'ctx'=4,'hd'=4] {'hd'}, dimensions={0}, use_global_device_ids=true | all-gather | bytes 327680 | tf_op jit(solution)/shard_map/all_gather | solution.py:198
  246.7 11.8 all-gather.1
  287.7 14.5 %all-to-all-start.5 = ((bf16[4,128,768]{1,2,0:T(8,128)(2,1)}), bf16[4,128,768]{1,2,0:T(8,128)(2,1)}, u32[]{:S(2)}, u32[]{:S(2)}) async-start(bf16[4,128,768]{1,2,0:T(8,128)(2,1)} %copy.489), calls=%async_computation.5 | async-start | bytes 1572864 | tf_op jit(solution)/shard_map/all_to_all | solution.py:221
  311.3 7.7 while.154
  320.1 11.6 all-gather
  398.9 9.2 multiply_reduce_fusion.13
  415.4 9.1 multiply_convert_fusion.3
  473.7 10.7 all-gather.3
  495.1 7.8 while.153
  515.9 11.2 all-gather.2
  653.6 8.2 reduce-scatter.7.cloned.1.call-done
  666.1 16.4 %reduce-scatter.5.cloned.1.call-done = bf16[128,256]{1,0:T(8,128)(2,1)} async-done(((bf16[512,256]{1,0:T(8,128)(2,1)}), bf16[128,256]{1,0:T(8,128)(2,1)}) %reduce-scatter.5.cloned.1.call-update) | async-done | bytes 65552 | tf_op jit(solution)/shard_map/reduce_scatter | solution.py:335
  698.8 19.9 %fusion.38 = f32[1536,6448]{1,0:T(8,128)} fusion(bf16[128,48]{1,0:T(8,128)(2,1)S(1)} %copy.558, bf16[128,3328]{1,0:T(8,128)(2,1)S(1)} %fusion.94, bf16[128,3072]{1,0:T(8,128)(2,1)S(1)} %copy-done.27, bf16[128,48]{1,0:T(8,128)(2,1)S(1)} %copy.557, bf16[128,3328]{1,0:T(8,128)(2,1)S(1)} %fusion.95, bf16[128,3072]{1,0:T(8,128)(2,1)} %get-tuple-element.1175, ...), kind=kOutput, calls=%fused_computation.78 | convolution fusion | flops 5092294656 | bytes 43704320 | tf_op jit(solution)/shard_map/dot_general | solution.py:384
  721.3 7.9 fusion.272
  729.2 9.6 fusion.270
  745.5 8.9 convolution_add_fusion.2
  755.8 8.9 convolution_add_fusion.3
  767.0 12.1 fusion.106
  793.6 293.1 %reduce-scatter.9.cloned.1.call-done = f32[48,6448]{1,0:T(8,128)} async-done(((f32[1536,6448]{1,0:T(8,128)}), f32[48,6448]{1,0:T(8,128)}) %reduce-scatter.9.cloned.1.call-update) | async-done | bytes 1238032 | tf_op jit(solution)/shard_map/reduce_scatter | solution.py:383
  1091.9 125.0 %all-reduce.31.cloned.1.call-done = (f32[1536]{0:T(1024)}, f32[4,3328]{1,0:T(4,128)}, f32[3328]{0:T(1024)}, f32[48]{0:T(128)}, f32[48]{0:T(128)}, /*index=5*/f32[48]{0:T(128)}, f32[3072]{0:T(1024)}) async-done(((f32[1536]{0:T(1024)}, f32[4,3328]{1,0:T(4,128)}, f32[3328]{0:T(1024)}, f32[48]{0:T(128)}, f32[48]{0:T(128)}, /*index=5*/f32[48]{0:T(128)}, f32[3072]{0:T(1024)}), (f32[1536]{0:T(1024)}, ...) | async-done | bytes 85584 | tf_op jit(solution)/shard_map/psum | solution.py:400
  1216.9 214.8 %reduce-scatter.11.cloned.1.call-done = f32[96,1536]{1,0:T(8,128)} async-done(((f32[3072,1536]{1,0:T(8,128)}), f32[96,1536]{1,0:T(8,128)}) %reduce-scatter.11.cloned.1.call-update) | async-done | bytes 589840 | tf_op jit(solution)/shard_map/reduce_scatter | solution.py:392
  (835 shorter events, 542.6 us)
Async XLA Ops:
  7.2 146.6 %all-gather.10.cloned.1.call-start = ((), (), s32[]{:S(2)}) async-start(), calls=%async_computation.14 | async-start | bytes 10543104 | tf_op jit(solution)/shard_map/all_gather | solution.py:162
  7.9 383.1 %all-gather.12.cloned.1.call-start = ((), (), s32[]{:S(2)}) async-start(), calls=%async_computation.15 | async-start | bytes 9732096 | tf_op jit(solution)/shard_map/all_gather | solution.py:161
  88.6 16.3 %all-to-all-start.4 = ((bf16[128,4,12]{0,2,1:T(8,128)(2,1)}), bf16[128,4,12]{0,2,1:T(8,128)(2,1)S(1)}, u32[]{:S(2)}, u32[]{:S(2)}) async-start(bf16[128,4,12]{0,2,1:T(8,128)(2,1)} %all_to_all.113), calls=%async_computation.4 | async-start | bytes 32768 | tf_op jit(solution)/shard_map/all_to_all | solution.py:196
  91.8 307.0 %all-gather.14.cloned.1.call-start = ((), (), s32[]{:S(2)}) async-start(), calls=%async_computation.16 | async-start | bytes 9732096 | tf_op jit(solution)/shard_map/all_gather | solution.py:164
  165.5 13.0 collective-permute-start
  173.0 51.1 %all-to-all-start.3 = ((bf16[128,4,768]{2,0,1:T(8,128)(2,1)}), bf16[128,4,768]{2,0,1:T(8,128)(2,1)}, u32[]{:S(2)}, u32[]{:S(2)}) async-start(bf16[128,4,768]{2,0,1:T(8,128)(2,1)} %bitcast.580), calls=%async_computation.3 | async-start | bytes 1572864 | tf_op jit(solution)/shard_map/all_to_all | solution.py:195
  224.1 63.6 %all-to-all-start = ((bf16[128,4,768]{2,0,1:T(8,128)(2,1)}), bf16[128,4,768]{2,0,1:T(8,128)(2,1)}, u32[]{:S(2)}, u32[]{:S(2)}) async-start(bf16[128,4,768]{2,0,1:T(8,128)(2,1)} %bitcast.579), calls=%async_computation | async-start | bytes 1572864 | tf_op jit(solution)/shard_map/all_to_all | solution.py:195
  287.7 79.3 %all-to-all-start.5 = ((bf16[4,128,768]{1,2,0:T(8,128)(2,1)}), bf16[4,128,768]{1,2,0:T(8,128)(2,1)}, u32[]{:S(2)}, u32[]{:S(2)}) async-start(bf16[4,128,768]{1,2,0:T(8,128)(2,1)} %copy.489), calls=%async_computation.5 | async-start | bytes 1572864 | tf_op jit(solution)/shard_map/all_to_all | solution.py:221
  366.9 18.6 %all-to-all-start.2 = ((bf16[4,128,768]{1,2,0:T(8,128)(2,1)}), bf16[4,128,768]{1,2,0:T(8,128)(2,1)}, u32[]{:S(2)}, u32[]{:S(2)}) async-start(bf16[4,128,768]{1,2,0:T(8,128)(2,1)} %copy.473), calls=%async_computation.2 | async-start | bytes 1572864 | tf_op jit(solution)/shard_map/all_to_all | solution.py:221
  431.0 15.9 %collective-permute-start.6 = (bf16[128,768]{1,0:T(8,128)(2,1)}, bf16[128,768]{1,0:T(8,128)(2,1)}, u32[]{:S(2)}, u32[]{:S(2)}) collective-permute-start(bf16[128,768]{1,0:T(8,128)(2,1)} %get-tuple-element.1200), channel_id=1, source_target_pairs={{0,1},{1,0},{2,3},{3,2},{4,5},{5,4},{6,7},{7,6},{8,9},{9,8},{10,11... | collective-permute-start | bytes 589832 | tf_op jit(solution)/shard_map/ppermute | solution.py:293
  438.0 18.2 %collective-permute-start.7 = (bf16[128,768]{1,0:T(8,128)(2,1)}, bf16[128,768]{1,0:T(8,128)(2,1)S(1)}, u32[]{:S(2)}, u32[]{:S(2)}) collective-permute-start(bf16[128,768]{1,0:T(8,128)(2,1)} %get-tuple-element.1199), channel_id=1, source_target_pairs={{0,2},{1,3},{2,0},{3,1},{4,6},{5,7},{6,4},{7,5},{8,10},{9,11},{10,... | collective-permute-start | bytes 589832 | tf_op jit(solution)/shard_map/ppermute | solution.py:293
  440.4 16.5 %collective-permute-start.8 = (bf16[128,768]{1,0:T(8,128)(2,1)}, bf16[128,768]{1,0:T(8,128)(2,1)S(1)}, u32[]{:S(2)}, u32[]{:S(2)}) collective-permute-start(bf16[128,768]{1,0:T(8,128)(2,1)} %get-tuple-element.1198), channel_id=1, source_target_pairs={{0,3},{1,2},{2,1},{3,0},{4,7},{5,6},{6,5},{7,4},{8,11},{9,10},{10,... | collective-permute-start | bytes 589832 | tf_op jit(solution)/shard_map/ppermute | solution.py:293
  442.7 19.8 %collective-permute-start.2 = (bf16[128,768]{1,0:T(8,128)(2,1)}, bf16[128,768]{1,0:T(8,128)(2,1)}, u32[]{:S(2)}, u32[]{:S(2)}) collective-permute-start(bf16[128,768]{1,0:T(8,128)(2,1)} %get-tuple-element.1196), channel_id=1, source_target_pairs={{0,1},{1,0},{2,3},{3,2},{4,5},{5,4},{6,7},{7,6},{8,9},{9,8},{10,11... | collective-permute-start | bytes 589832 | tf_op jit(solution)/shard_map/ppermute | solution.py:293
  443.7 19.8 %collective-permute-start.3 = (bf16[128,768]{1,0:T(8,128)(2,1)}, bf16[128,768]{1,0:T(8,128)(2,1)}, u32[]{:S(2)}, u32[]{:S(2)}) collective-permute-start(bf16[128,768]{1,0:T(8,128)(2,1)} %get-tuple-element.1195), channel_id=1, source_target_pairs={{0,2},{1,3},{2,0},{3,1},{4,6},{5,7},{6,4},{7,5},{8,10},{9,11},{10,... | collective-permute-start | bytes 589832 | tf_op jit(solution)/shard_map/ppermute | solution.py:293
  447.0 17.4 %collective-permute-start.4 = (bf16[128,768]{1,0:T(8,128)(2,1)}, bf16[128,768]{1,0:T(8,128)(2,1)}, u32[]{:S(2)}, u32[]{:S(2)}) collective-permute-start(bf16[128,768]{1,0:T(8,128)(2,1)} %get-tuple-element.1194), channel_id=1, source_target_pairs={{0,3},{1,2},{2,1},{3,0},{4,7},{5,6},{6,5},{7,4},{8,11},{9,10},{10,... | collective-permute-start | bytes 589832 | tf_op jit(solution)/shard_map/ppermute | solution.py:293
  578.9 10.8 all-to-all-start.9
  589.7 16.9 %all-to-all-start.7 = ((bf16[4,128,12]{1,2,0:T(8,128)(2,1)}), bf16[4,128,12]{1,2,0:T(8,128)(2,1)S(1)}, u32[]{:S(2)}, u32[]{:S(2)}) async-start(bf16[4,128,12]{1,2,0:T(8,128)(2,1)} %copy.523), calls=%async_computation.8 | async-start | bytes 32768 | tf_op jit(solution)/shard_map/all_to_all | solution.py:331
  606.6 26.6 %all-to-all-start.8 = ((bf16[4,128,768]{1,2,0:T(8,128)(2,1)}), bf16[4,128,768]{1,2,0:T(8,128)(2,1)}, u32[]{:S(2)}, u32[]{:S(2)}) async-start(bf16[4,128,768]{1,2,0:T(8,128)(2,1)} %copy.539), calls=%async_computation.9 | async-start | bytes 1572864 | tf_op jit(solution)/shard_map/all_to_all | solution.py:328
  633.2 18.9 %all-to-all-start.6 = ((bf16[4,128,768]{1,2,0:T(8,128)(2,1)}), bf16[4,128,768]{1,2,0:T(8,128)(2,1)}, u32[]{:S(2)}, u32[]{:S(2)}) async-start(bf16[4,128,768]{1,2,0:T(8,128)(2,1)} %copy.506), calls=%async_computation.6 | async-start | bytes 1572864 | tf_op jit(solution)/shard_map/all_to_all | solution.py:328
  638.3 23.5 %reduce-scatter.7.cloned.1.call-start = ((), (), s32[]{:S(2)}) async-start(), calls=%async_computation.18 | async-start | bytes 327680 | tf_op jit(solution)/shard_map/reduce_scatter | solution.py:335
  639.5 43.0 %reduce-scatter.5.cloned.1.call-start = ((), (), s32[]{:S(2)}) async-start(), calls=%async_computation.17 | async-start | bytes 327680 | tf_op jit(solution)/shard_map/reduce_scatter | solution.py:335
  649.5 437.2 %reduce-scatter.9.cloned.1.call-start = ((), (), s32[]{:S(2)}) async-start(), calls=%async_computation.19 | async-start | bytes 41361408 | tf_op jit(solution)/shard_map/reduce_scatter | solution.py:383
  718.7 498.3 %all-reduce.31.cloned.1.call-start = ((), (), s32[]{:S(2)}) async-start(), calls=%async_computation.21 | async-start | bytes 183296 | tf_op jit(solution)/shard_map/psum | solution.py:400
  766.9 664.8 %reduce-scatter.11.cloned.1.call-start = ((), (), s32[]{:S(2)}) async-start(), calls=%async_computation.20 | async-start | bytes 19464192 | tf_op jit(solution)/shard_map/reduce_scatter | solution.py:392
  (176 other events, 1923.2 us)
Sparse Core Ops, SparseCore 0:
  10.8 90.7 all-gather.9
  104.4 91.1 all-gather.11
  198.5 93.4 all-gather.13
  641.7 20.1 reduce-scatter.6
  664.6 17.8 reduce-scatter.4
  718.8 367.8 reduce-scatter.8
  1094.3 122.6 all-reduce.30
  1223.9 207.8 reduce-scatter.10
